TPU v7x, 256 devices: a whole 4x4x8 slice. The times are simulated.
256 devices in a mesh: dp: 16 (over x, y), tensor: 16 (over z, core).
Axes of the slice: x: 4, y: 4, z: 8, core: 2. Of those that a mesh axis runs over, the one named last changes fastest.
Arguments:
- out_grad: bfloat16 [12288, 8192], P('dp', 'tensor'), may hold values from -6 to 6
- block_input: bfloat16 [12288, 8192], P('dp', 'tensor'), may hold values from -6 to 6
- gate_pre: bfloat16 [12288, 14336], P('dp', 'tensor'), may hold values from -8 to 8
- up_pre: bfloat16 [12288, 14336], P('dp', 'tensor'), may hold values from -6 to 6
- down_weight: bfloat16 [14336, 8192], P('tensor', 'dp'), may hold values from -0.046875 to 0.046875
- gate_in: bfloat16 [48, 16, 8192], P(None, None, 'tensor'), may hold values from -0.0625 to 0.0625
- gate_adapter_output_maps: bfloat16 [48, 16, 14336], P(None, None, 'tensor'), may hold values from -0.046875 to 0.046875
- up_in: bfloat16 [48, 16, 8192], P(None, None, 'tensor'), may hold values from -0.0625 to 0.0625
- up_adapter_output_maps: bfloat16 [48, 16, 14336], P(None, None, 'tensor'), may hold values from -0.046875 to 0.046875
- down_in: bfloat16 [48, 16, 14336], P(None, None, 'tensor'), may hold values from -0.046875 to 0.046875
- down_out: bfloat16 [48, 16, 8192], P(None, None, 'tensor'), may hold values from -0.0625 to 0.0625
- block_adapter: int32 [96], replicated, may hold values from 0 to 47, as said below
- owned_ids: int32 [48], replicated, may hold values from 0 to 47, as said below
Outputs:
- input_grad: bfloat16 [12288, 8192], P('dp', 'tensor')
- grad_gate_in: float32 [48, 16, 8192], P('dp', None, 'tensor')
- grad_gate_out: float32 [48, 16, 14336], P('dp', None, 'tensor')
- grad_up_in: float32 [48, 16, 8192], P('dp', None, 'tensor')
- grad_up_out: float32 [48, 16, 14336], P('dp', None, 'tensor')
- grad_down_in: float32 [48, 16, 14336], P('dp', None, 'tensor')
- grad_down_out: float32 [48, 16, 8192], P('dp', None, 'tensor')
Inputs may be any that keep to these rules, and one draw needn't show every extreme that they name: `block_adapter`: replica q (blocks q * 6 to q * 6 + 5) owns the adapters owned_ids[q * 3] to owned_ids[q * 3 + 2]. Among the 6 blocks of one replica, at most 1 names an adapter of any one owner; in every draw each replica has some owner that it names exactly once. `owned_ids`: each adapter appears once.
All inputs are finite; a program needn't handle non-finite values.
Results may differ from a plain program's by a relative error of at most 0.0058.
Values may be sent and summed in bfloat16 or wider, within the bound.
A program may use at most 128 MiB of HBM per device.

v0:
```python
import jax
import jax.numpy as jnp
from jax import lax
from jax.sharding import PartitionSpec as P

adapter_scale_factor = 2.0


def apply_projection(left, table):
    return jnp.einsum("nbd,nrd->nrb", left, table, preferred_element_type=jnp.float32)


def outer_product_sum(low, right):
    return jnp.einsum("nrb,nbw->nrw", low, right, preferred_element_type=jnp.float32)


def shards(
    out_grad,
    block_input,
    gate_pre,
    up_pre,
    down_weight,
    gate_in,
    gate_adapter_output_maps,
    up_in,
    up_adapter_output_maps,
    down_in,
    down_out,
    block_adapter,
    owned_ids,
):
    replicas = lax.axis_size("dp")
    replica = lax.axis_index("dp")
    tok_rows, width_part = out_grad.shape
    hidden_width_slice = gate_pre.shape[1]
    blocks_all = block_adapter.reshape(replicas, -1)
    block_count = blocks_all.shape[1]
    rows_per_block = tok_rows // block_count
    adapters = owned_ids.shape[0]
    owned = adapters // replicas
    capacity = (block_count + replicas - 1) // replicas
    my_ids = lax.dynamic_index_in_dim(blocks_all, replica, 0, keepdims=False)
    g_in = jnp.take(gate_in, my_ids, axis=0)
    gate_output_grad = jnp.take(gate_adapter_output_maps, my_ids, axis=0)
    u_in = jnp.take(up_in, my_ids, axis=0)
    up_output_grad = jnp.take(up_adapter_output_maps, my_ids, axis=0)
    input_dimension = jnp.take(down_in, my_ids, axis=0)
    d_out = jnp.take(down_out, my_ids, axis=0)
    output_grad_blocks = out_grad.reshape(block_count, rows_per_block, width_part)
    input_blocks = block_input.reshape(block_count, rows_per_block, width_part)
    gate_f = gate_pre.reshape(block_count, rows_per_block, hidden_width_slice).astype(jnp.float32)
    up_f = up_pre.reshape(block_count, rows_per_block, hidden_width_slice).astype(jnp.float32)
    hidden_activation = (jax.nn.silu(gate_f) * up_f).astype(jnp.bfloat16)
    partials = (
        apply_projection(input_blocks, g_in),
        apply_projection(input_blocks, u_in),
        apply_projection(hidden_activation, input_dimension),
        apply_projection(output_grad_blocks, d_out),
    )
    reduced = lax.psum((partials[0], partials[1], partials[2], partials[3]), "tensor")
    rank_gate_projection = reduced[0].astype(jnp.bfloat16)
    rank_up_projection = reduced[1].astype(jnp.bfloat16)
    rank_down_projection = reduced[2].astype(jnp.bfloat16)
    down_error_signal = reduced[3].astype(jnp.bfloat16)
    dy_full = lax.all_gather(out_grad, "tensor", axis=1, tiled=True)
    frozen_base_output = lax.dot_general(
        dy_full,
        lax.all_gather(down_weight, "dp", axis=1, tiled=True),
        (((1,), (1,)), ((), ())),
        preferred_element_type=jnp.float32,
    )
    hidden_gradient_rows = frozen_base_output.reshape(
        block_count, rows_per_block, hidden_width_slice
    ) + adapter_scale_factor * jnp.einsum(
        "elz,elp->ezp", down_error_signal, input_dimension, preferred_element_type=jnp.float32
    )
    sigmoid_gate = jax.nn.sigmoid(gate_f)
    gate_gradient_total = (
        hidden_gradient_rows * up_f * sigmoid_gate * (1.0 + gate_f * (1.0 - sigmoid_gate))
    ).astype(jnp.bfloat16)
    up_gradient_total = (hidden_gradient_rows * gate_f * sigmoid_gate).astype(jnp.bfloat16)
    returned = lax.psum(
        (
            adapter_scale_factor * apply_projection(gate_gradient_total, gate_output_grad),
            adapter_scale_factor * apply_projection(up_gradient_total, up_output_grad),
        ),
        "tensor",
    )
    gate_backward = returned[0].astype(jnp.bfloat16)
    up_backward = returned[1].astype(jnp.bfloat16)
    input_grad = jnp.einsum(
        "nrb,nrd->nbd", gate_backward, g_in, preferred_element_type=jnp.float32
    ) + jnp.einsum("nrb,nrd->nbd", up_backward, u_in, preferred_element_type=jnp.float32)
    input_grad = input_grad.astype(jnp.bfloat16).reshape(tok_rows, width_part)
    packet = jnp.concatenate(
        [
            outer_product_sum(gate_backward, input_blocks),
            adapter_scale_factor * outer_product_sum(rank_gate_projection, gate_gradient_total),
            outer_product_sum(up_backward, input_blocks),
            adapter_scale_factor * outer_product_sum(rank_up_projection, up_gradient_total),
            adapter_scale_factor * outer_product_sum(down_error_signal, hidden_activation),
            adapter_scale_factor * outer_product_sum(rank_down_projection, output_grad_blocks),
        ],
        axis=2,
    )
    order_index = jnp.arange(adapters, dtype=jnp.int32)
    rank_of = jnp.sum(
        jnp.where(owned_ids[None, :] == order_index[:, None], order_index[None, :], 0), axis=1
    )
    position = jnp.take(rank_of, blocks_all)
    target_all = position // owned
    local_all = position % owned
    block_index = jnp.arange(block_count, dtype=jnp.int32)
    earlier = block_index[:, None] > block_index[None, :]
    same_target = target_all[:, :, None] == target_all[:, None, :]
    slot_all = jnp.sum(jnp.logical_and(same_target, earlier[None, :, :]).astype(jnp.int32), axis=2)
    my_target = lax.dynamic_index_in_dim(target_all, replica, 0, keepdims=False)
    my_slot = lax.dynamic_index_in_dim(slot_all, replica, 0, keepdims=False)
    replica_index = jnp.arange(replicas, dtype=jnp.int32)
    slot_index = jnp.arange(capacity, dtype=jnp.int32)
    owned_index = jnp.arange(owned, dtype=jnp.int32)
    send_table = jnp.logical_and(
        my_target[None, None, :] == replica_index[:, None, None],
        my_slot[None, None, :] == slot_index[None, :, None],
    ).astype(jnp.float32)
    outgoing = jnp.einsum("qcn,nrw->qcrw", send_table, packet, precision=lax.Precision.HIGHEST)
    mine = (target_all == replica)[:, None, :, None]
    slot_match = slot_all[:, None, :, None] == slot_index[None, :, None, None]
    local_match = local_all[:, None, :, None] == owned_index[None, None, None, :]
    receive_table = jnp.sum(
        jnp.logical_and(jnp.logical_and(mine, slot_match), local_match).astype(jnp.float32), axis=2
    )
    owned_grads = jnp.einsum(
        "qco,qckw->okw",
        receive_table,
        lax.all_to_all(
            outgoing.astype(jnp.bfloat16), "dp", split_axis=0, concat_axis=0, tiled=True
        ).astype(outgoing.dtype),
        precision=lax.Precision.HIGHEST,
    )
    second = width_part + hidden_width_slice
    third = second + width_part
    fourth = third + hidden_width_slice
    fifth = fourth + hidden_width_slice
    return (
        input_grad,
        owned_grads[:, :, :width_part],
        owned_grads[:, :, width_part:second],
        owned_grads[:, :, second:third],
        owned_grads[:, :, third:fourth],
        owned_grads[:, :, fourth:fifth],
        owned_grads[:, :, fifth:],
    )


def solution(mesh):
    in_specs = (
        P("dp", "tensor"),
        P("dp", "tensor"),
        P("dp", "tensor"),
        P("dp", "tensor"),
        P("tensor", "dp"),
        P(None, None, "tensor"),
        P(None, None, "tensor"),
        P(None, None, "tensor"),
        P(None, None, "tensor"),
        P(None, None, "tensor"),
        P(None, None, "tensor"),
        P(),
        P(),
    )
    out_specs = (
        P("dp", "tensor"),
        P("dp", None, "tensor"),
        P("dp", None, "tensor"),
        P("dp", None, "tensor"),
        P("dp", None, "tensor"),
        P("dp", None, "tensor"),
        P("dp", None, "tensor"),
    )
    return jax.shard_map(shards, mesh=mesh, in_specs=in_specs, out_specs=out_specs, check_vma=False)
```

profile of v0, /device:TPU:1, one launch (start us, length us, event | category | flops | bytes accessed | tf_op | source)
XLA Modules:
  0.0 326.1 jit_solution(10830039742640613778)
XLA Ops:
  7.2 0.7 all-gather.3.cloned.1.call-update
  8.0 0.7 all-gather.5.cloned.1.call-update
  9.2 1.2 gather_fusion
  10.7 0.7 dynamic-slice_reduce_fusion
  11.4 1.7 gather_fusion.6
  13.4 1.7 gather_fusion.4
  15.1 1.0 fusion.30
  16.1 2.3 gather_fusion.2
  18.5 1.2 gather_fusion.3
  19.7 1.9 gather_fusion.5
  21.6 1.9 gather_fusion.1
  23.6 0.7 fusion.47
  24.4 1.3 fusion.23
  25.6 54.8 %psum.42 = bf16[6,16,128]{2,1,0:T(8,128)(2,1)S(1)} all-reduce(f32[6,16,128]{2,1,0:T(8,128)S(1)} %fusion.23), channel_id=1, replica_groups=mesh['dp'=16,'tensor'=16] {'tensor'}, use_global_device_ids=true, to_apply=%region_0.0 | all-reduce | flops 12288 | bytes 73728 | tf_op jit(solution)/shard_map/psum | solution.py:60
  80.4 10.0 %all-gather.3.cloned.1.call-done = bf16[768,8192]{1,0:T(8,128)(2,1)} async-done(((bf16[768,512]{1,0:T(8,128)(2,1)}), bf16[768,8192]{1,0:T(8,128)(2,1)}) %all-gather.3.cloned.1.call-update) | async-done | bytes 12582928 | tf_op jit(solution)/shard_map/all_gather | solution.py:65
  90.4 113.3 %all-gather.5.cloned.1.call-done = bf16[896,8192]{1,0:T(8,128)(2,1)} async-done(((bf16[896,512]{1,0:T(8,128)(2,1)}), bf16[896,8192]{1,0:T(8,128)(2,1)}) %all-gather.5.cloned.1.call-update) | async-done | bytes 14680080 | tf_op jit(solution)/shard_map/all_gather | solution.py:68
  203.8 17.9 %fusion.63 = f32[768,896]{1,0:T(8,128)S(1)} fusion(bf16[768,8192]{1,0:T(8,128)(2,1)} %all-gather.3.cloned.1.call-done, bf16[896,8192]{1,0:T(8,128)(2,1)} %all-gather.5.cloned.1.call-done), kind=kOutput, calls=%fused_computation.110 | convolution fusion | flops 11274289152 | bytes 30015488 | tf_op jit(solution)/shard_map/dot_general | solution.py:66
  221.8 2.2 fusion.10
  224.0 1.1 copy-done.3
  226.8 47.9 %all-reduce.2 = (bf16[6,16,128]{2,1,0:T(8,128)(2,1)S(1)}, bf16[6,16,128]{2,1,0:T(8,128)(2,1)S(1)}, bf16[6,16,128]{2,1,0:T(8,128)(2,1)S(1)}, bf16[6,16,128]{2,1,0:T(8,128)(2,1)S(1)}, bf16[6,16,128]{2,1,0:T(8,128)(2,1)S(1)}) all-reduce(f32[6,16,128]{2,1,0:T(8,128)S(1)} %convolution_multiply_fusion.5,, ...), channel_id=1, replica_groups=mesh['dp'=16,'tensor'=16] {'tensor'}, use_global_device_ids=true, to_apply=%region_1.4 | all-reduce | flops 61440 | bytes 368640 | tf_op jit(solution)/shard_map/psum | solution.py:82
  275.3 1.7 fusion.17
  277.6 0.8 copy-done.4
  279.1 2.6 fusion
  281.7 1.7 copy.59
  283.4 4.7 %all-to-all-start = ((bf16[16,1,16,4224]{3,2,1,0:T(8,128)(2,1)}), bf16[16,1,16,4224]{3,2,1,0:T(8,128)(2,1)S(1)}, u32[]{:S(2)}, u32[]{:S(2)}) async-start(bf16[16,1,16,4224]{3,2,1,0:T(8,128)(2,1)} %copy.59), calls=%async_computation | async-start | bytes 4325376 | tf_op jit(solution)/shard_map/all_to_all | solution.py:136
  288.1 1.3 fusion.31
  289.5 1.3 add_convert_fusion
  290.8 23.0 %all-to-all-done = bf16[16,1,16,4224]{3,2,1,0:T(8,128)(2,1)S(1)} async-done(((bf16[16,1,16,4224]{3,2,1,0:T(8,128)(2,1)}), bf16[16,1,16,4224]{3,2,1,0:T(8,128)(2,1)S(1)}, u32[]{:S(2)}, u32[]{:S(2)}) %all-to-all-start) | async-done | bytes 2162720 | tf_op jit(solution)/shard_map/all_to_all | solution.py:136
  313.8 1.1 fusion.11
  315.2 0.7 copy.65
  317.9 0.7 copy.64
  318.5 0.7 copy.62
  (77 shorter events, 7.0 us)
Async XLA Ops:
  7.2 11.3 %copy-start = (bf16[48,16,896]{2,1,0:T(8,128)(2,1)S(1)}, bf16[48,16,896]{2,1,0:T(8,128)(2,1)}, u32[]{:S(2)}) copy-start(bf16[48,16,896]{2,1,0:T(8,128)(2,1)} %param.26) | copy-start | bytes 4128772
  7.2 1.5 copy-start.20
  7.2 1.9 copy-start.23
  7.2 83.2 %all-gather.3.cloned.1.call-start = ((), (), s32[]{:S(2)}) async-start(), calls=%async_computation.1 | async-start | bytes 13369344 | tf_op jit(solution)/shard_map/all_gather | solution.py:65
  7.9 195.8 %all-gather.5.cloned.1.call-start = ((), (), s32[]{:S(2)}) async-start(), calls=%async_computation.2 | async-start | bytes 15597568 | tf_op jit(solution)/shard_map/all_gather | solution.py:68
  9.2 3.8 %copy-start.1 = (bf16[768,512]{1,0:T(8,128)(2,1)S(1)}, bf16[768,512]{1,0:T(8,128)(2,1)}, u32[]{:S(2)}) copy-start(bf16[768,512]{1,0:T(8,128)(2,1)} %param.18) | copy-start | bytes 2359300
  13.0 10.5 %copy-start.8 = (bf16[6,16,512]{2,1,0:T(8,128)(2,1)}, bf16[6,16,512]{2,1,0:T(8,128)(2,1)S(1)}, u32[]{:S(2)}) copy-start(bf16[6,16,512]{2,1,0:T(8,128)(2,1)S(1)} %gather_fusion.6) | copy-start | bytes 294916
  13.1 11.3 %copy-start.2 = (bf16[768,512]{1,0:T(8,128)(2,1)S(1)}, bf16[768,512]{1,0:T(8,128)(2,1)}, u32[]{:S(2)}) copy-start(bf16[768,512]{1,0:T(8,128)(2,1)} %param.17) | copy-start | bytes 2359300
  15.1 206.6 %copy-start.10 = (bf16[6,16,512]{2,1,0:T(8,128)(2,1)}, bf16[6,16,512]{2,1,0:T(8,128)(2,1)S(1)}, u32[]{:S(2)}) copy-start(bf16[6,16,512]{2,1,0:T(8,128)(2,1)S(1)} %gather_fusion.4) | copy-start | bytes 294916
  80.4 141.3 %copy-start.15 = (bf16[6,16,128]{2,1,0:T(8,128)(2,1)}, bf16[6,16,128]{2,1,0:T(8,128)(2,1)S(1)}, u32[]{:S(2)}) copy-start(bf16[6,16,128]{2,1,0:T(8,128)(2,1)S(1)} %psum.42) | copy-start | bytes 73732
  203.8 18.0 %copy-start.11 = (bf16[6,16,896]{2,1,0:T(8,128)(2,1)S(1)}, bf16[6,16,896]{2,1,0:T(8,128)(2,1)}, u32[]{:S(2)}) copy-start(bf16[6,16,896]{2,1,0:T(8,128)(2,1)} %gather_fusion.3) | copy-start | bytes 516100
  203.8 18.0 %copy-start.21 = (bf16[768,896]{1,0:T(8,128)(2,1)S(1)}, bf16[768,896]{1,0:T(8,128)(2,1)}, u32[]{:S(2)}) copy-start(bf16[768,896]{1,0:T(8,128)(2,1)} %param.19) | copy-start | bytes 4128772
  203.8 18.0 %copy-start.22 = (bf16[768,896]{1,0:T(8,128)(2,1)S(1)}, bf16[768,896]{1,0:T(8,128)(2,1)}, u32[]{:S(2)}) copy-start(bf16[768,896]{1,0:T(8,128)(2,1)} %param.20) | copy-start | bytes 4128772
  224.0 1.1 copy-start.3
  224.0 1.6 copy-start.5
  224.0 2.2 copy-start.7
  225.6 1.1 copy-start.12
  274.7 0.6 copy-start.17
  274.7 2.5 copy-start.13
  275.0 2.3 copy-start.6
  277.0 1.3 copy-start.4
  277.0 1.4 copy-start.16
  278.4 0.7 copy-start.18
  278.4 0.7 copy-start.19
  283.4 30.4 %all-to-all-start = ((bf16[16,1,16,4224]{3,2,1,0:T(8,128)(2,1)}), bf16[16,1,16,4224]{3,2,1,0:T(8,128)(2,1)S(1)}, u32[]{:S(2)}, u32[]{:S(2)}) async-start(bf16[16,1,16,4224]{3,2,1,0:T(8,128)(2,1)} %copy.59), calls=%async_computation | async-start | bytes 4325376 | tf_op jit(solution)/shard_map/all_to_all | solution.py:136
  288.1 1.4 copy-start.9
  288.1 1.4 copy-start.14
Sparse Core Ops, SparseCore 0:
  9.9 80.5 all-gather.2
  92.8 110.8 all-gather.4
where the time goes:
time: 331 us; the launch traced here: 326 us
  waiting for transfers between devices  148 us (45%)
  blocking collectives  103 us (31%)
  matrix products  33.8 us (10%)
  local copies, waits for them, and re-layouts  21.6 us (7%)
  between operations  14.4 us (4%)
  starting transfers between devices  4.74 us (1%)
    all_gather x1, waiting for transfers between devices, shards(): lax.all_gather(down_weight, 'dp', axis=1, tiled=True)  113 us
    psum x1, blocking collectives, shards(): lax.psum((partials[0], partials[1], partials[2], partials[3]), 'tensor')  54.8 us
    psum x1, blocking collectives, shards(): lax.psum((adapter_scale_factor * apply_projection(gate_gradient_total, ga...  47.9 us
    all_to_all x1, waiting for transfers between devices, shards(): lax.all_to_all(outgoing.astype(jnp.bfloat16), 'dp', split_axis=0, concat_...  23 us
    dot_general x1, matrix products, shards(): lax.dot_general(dy_full, lax.all_gather(down_weight, 'dp', axis=1, tiled=...  17.9 us
    all_gather x1, waiting for transfers between devices, shards(): dy_full = lax.all_gather(out_grad, 'tensor', axis=1, tiled=True)  9.99 us
  transfers between devices with their start and end apart: 3, of which 3 were waited for; matrix products, arithmetic and copies ran while one was open for 6% of the time, Pallas kernels for 0%

commit v1 on v0

v1 whole, which is shorter than its diff:
```python
import heapq

import jax
import jax.numpy as jnp
from jax import lax
from jax.experimental import pallas as pl
from jax.experimental.pallas import tpu as pltpu
from jax.sharding import PartitionSpec as P

SCALE = 2.0
F32 = jnp.float32
BF16 = jnp.bfloat16
MESH = pl.DeviceIdType.MESH
RING = 4
DEPTH = 8


def centred(a):
    return ((a + 1) % RING) - 1


def weight_hops(kind, u, v):
    sign = 1 if kind % 2 == 0 else -1
    first, second = ("x", "y") if kind < 2 else ("y", "x")
    hops = []
    if v == 0:
        if u == 0:
            hops += [(first, sign), (first, -sign)]
        elif u == -sign:
            hops += [(first, sign)]
        hops += [(second, sign), (second, -sign)]
    elif v == -sign:
        hops += [(second, sign)]
    return first, hops


def weight_timeline(unit):
    free = {(a, s): 0.0 for a in "xy" for s in (1, -1)}
    order, count = [], 0
    heap = [(0.0, k - 4, k, 0, 0) for k in range(4)]
    heapq.heapify(heap)
    while heap:
        now, _, kind, u, v = heapq.heappop(heap)
        order.append((now, kind, u, v))
        first, hops = weight_hops(kind, u, v)
        for axis, sign in hops:
            end = max(free[(axis, sign)], now) + unit
            free[(axis, sign)] = end
            nu, nv = (centred(u - sign), v) if axis == first else (u, centred(v - sign))
            heapq.heappush(heap, (end + 1.5, count, kind, nu, nv))
            count += 1
    return order


def rows_dot(a, b):
    return lax.dot_general(a, b, (((1,), (1,)), ((), ())), preferred_element_type=F32)


def turned_dot(a, b):
    return jnp.dot(a.astype(F32).T.astype(BF16), b, preferred_element_type=F32)


def kernel(
    dims,
    dy_h, x_h, gp_h, up_h, w_h, gin_h, gout_h, uin_h, uout_h, din_h, dout_h, ids, owned,
    ig_h, o_gin, o_gout, o_uin, o_uout, o_din, o_dout,
    dyf, wf, xb, gp, up, tw, tf, fa, fb, hid, acc, part1, red1, res1, part2, red2, res2, big, pick,
    s_d, s_o, s_i, r_d, r_o, r_i, ig, st_w, st_f,
    loc_sem, out_sem, dsend, drecv, csend, crecv, wsend, wrecv,
    rs1s, rs1r, ag1s, ag1r, rs2s, rs2r, ag2s, ag2r, a2s, a2r,
):
    NB, RB, WD, FW, NQ, NS, OWN, RK = dims
    q = lax.axis_index("dp")
    s = lax.axis_index("tensor")
    x, y = q // RING, q % RING
    z, c = s // 2, s % 2

    def dp_at(axis, sign):
        if axis == "x":
            return ((x + sign + RING) % RING) * RING + y
        return x * RING + (y + sign + RING) % RING

    def to_dp(qq):
        return {"dp": qq, "tensor": s}

    def to_tensor(ss):
        return {"dp": q, "tensor": ss}

    def z_at(off):
        return (z + off + DEPTH) % DEPTH

    def remote(src, dst, ss, rs, dev):
        return pltpu.make_async_remote_copy(
            src_ref=src, dst_ref=dst, send_sem=ss, recv_sem=rs, device_id=dev, device_id_type=MESH
        )

    loads = [
        (dy_h, dyf.at[s]), (x_h, xb), (gp_h, gp), (up_h, up), (w_h, wf.at[q]),
        (gin_h, tw.at[0]), (uin_h, tw.at[1]), (dout_h, tw.at[2]),
        (gout_h, tf.at[0]), (uout_h, tf.at[1]), (din_h, tf.at[2]),
    ]
    loads = [pltpu.make_async_copy(a, b, loc_sem.at[i]) for i, (a, b) in enumerate(loads)]

    barrier = pltpu.get_barrier_semaphore()
    peers = [to_dp(dp_at(a, sg)) for a in "xy" for sg in (1, -1)]
    peers += [to_tensor(z_at(1) * 2 + c), to_tensor(z_at(-1) * 2 + c), to_tensor(z * 2 + 1 - c)]
    for peer in peers:
        pl.semaphore_signal(barrier, inc=1, device_id=peer, device_id_type=MESH)
    pl.semaphore_wait(barrier, len(peers))

    QR = wf.shape[1] // 4
    wcount = [0]

    def wpiece(kind, u, v):
        ox, oy = (u, v) if kind < 2 else (v, u)
        qq = ((x + ox + RING) % RING) * RING + (y + oy + RING) % RING
        return wf.at[qq, pl.ds(kind * QR, QR), :]

    def wsem(kind, u, v):
        return kind * 16 + (u % RING) * RING + v % RING

    def wforward(kind, u, v):
        first, hops = weight_hops(kind, u, v)
        piece = wpiece(kind, u, v)
        src = w_h.at[pl.ds(kind * QR, QR), :] if (u, v) == (0, 0) else piece
        for axis, sign in hops:
            nu, nv = (centred(u - sign), v) if axis == first else (u, centred(v - sign))
            remote(
                src, piece, wsend.at[wcount[0]], wrecv.at[wsem(kind, nu, nv)], to_dp(dp_at(axis, sign))
            ).start()
            wcount[0] += 1

    def wwait(kind, u, v):
        piece = wpiece(kind, u, v)
        remote(piece, piece, wsend.at[0], wrecv.at[wsem(kind, u, v)], to_dp(q)).wait_recv()

    HR = dyf.shape[1] // 2
    dcount = [0]
    ccount = [0]

    def dpiece(off, h, core):
        return dyf.at[z_at(off) * 2 + core, pl.ds(h * HR, HR), :]

    def dsem(off, h):
        return (off % DEPTH) * 2 + h

    def dforward(off, h):
        piece = dpiece(off, h, c)
        src = dy_h.at[pl.ds(h * HR, HR), :] if off == 0 else piece
        going = []
        if off <= 0 and (off > -3 or (off == -3 and h == 0)):
            going.append(1)
        if off >= 0 and (off < 3 or (off == 3 and h == 1)):
            going.append(-1)
        for sign in going:
            to = off - sign
            remote(
                src, piece, dsend.at[dcount[0]], drecv.at[dsem(to, h)], to_tensor(z_at(sign) * 2 + c)
            ).start()
            dcount[0] += 1
        remote(
            src, piece, csend.at[ccount[0]], crecv.at[dsem(off, h)], to_tensor(z * 2 + 1 - c)
        ).start()
        ccount[0] += 1

    def dwait(off, h):
        piece = dpiece(off, h, c)
        remote(piece, piece, dsend.at[0], drecv.at[dsem(off, h)], to_tensor(s)).wait_recv()

    def cwait(off, h):
        piece = dpiece(off, h, 1 - c)
        remote(piece, piece, csend.at[0], crecv.at[dsem(off, h)], to_tensor(s)).wait_recv()

    for kind in range(4):
        wforward(kind, 0, 0)
    for h in range(2):
        dforward(0, h)
    for cp in loads:
        cp.start()

    ids_me = [ids[q * NB + n] for n in range(NB)]

    def rows(n):
        return pl.ds(n * RB, RB)

    def act(n):
        @pl.loop(0, RB // 16)
        def _(i):
            r = pl.ds(pl.multiple_of(n * RB + i * 16, 16), 16)
            g = gp[r, :].astype(F32)
            u = up[r, :].astype(F32)
            sg = jax.nn.sigmoid(g)
            b = g * sg
            fb[r, :] = b
            fa[r, :] = u * sg * (1.0 + g * (1.0 - sg))
            hid[r, :] = (b * u).astype(BF16)

    def ranks(n):
        a = ids_me[n]
        part1[n] = rows_dot(tw[0, a], xb[rows(n), :])
        part1[NB + n] = rows_dot(tw[1, a], xb[rows(n), :])
        part1[2 * NB + n] = rows_dot(tf[2, a], hid[rows(n), :])
        part1[3 * NB + n] = rows_dot(tw[2, a], dyf[s, rows(n), :])

    def picker():
        row = lax.broadcasted_iota(jnp.int32, (OWN * RK, NQ * RK), 0)
        col = lax.broadcasted_iota(jnp.int32, (OWN * RK, NQ * RK), 1)
        same = (row % RK) == (col % RK)
        rown, cown = row // RK, col // RK

        def body(qq, m):
            for o in range(OWN):
                mine = owned[q * OWN + o]
                hit = jnp.int32(0)
                for n in range(NB):
                    hit = hit + jnp.where(ids[qq * NB + n] == mine, 1, 0)
                val = jnp.where(hit > 0, 1.0, 0.0).astype(F32)
                m = m + jnp.where((cown == qq) & (rown == o) & same, 1.0, 0.0) * val
            return m

        pick[...] = lax.fori_loop(0, NQ, body, jnp.zeros((OWN * RK, NQ * RK), F32)).astype(BF16)

    def waits(a, b):
        def run():
            for cp in loads[a:b]:
                cp.wait()

        return run

    acc_rows = 256

    def product(ox, oy, fresh=False):
        k = ((x + ox + RING) % RING) * RING + (y + oy + RING) % RING

        @pl.loop(0, acc.shape[0] // acc_rows)
        def _(m):
            r = pl.ds(pl.multiple_of(m * acc_rows, acc_rows), acc_rows)
            d = rows_dot(dyf[k, r, :], wf[k])
            acc[r, :] = d if fresh else acc[r, :] + d

    def scatter(part, red, count, ssem, rsem):
        def one(t, _):
            to = (s + t) % NS
            for lane in range((count + NS - 1) // NS):
                def send(lane=lane, to=to):
                    remote(
                        part.at[lane * NS + to], red.at[lane, s], ssem.at[lane, t], rsem.at[lane, s], to_tensor(to)
                    ).start()
                if (lane + 1) * NS <= count:
                    send()
                else:
                    pl.when(to < count - lane * NS)(send)
            return 0

        lax.fori_loop(1, NS, one, 0)

    def gather_sum(part, red, res, count, rsem, ssem2, rsem2):
        for lane in range((count + NS - 1) // NS):
            def go(lane=lane):
                def wait(t, _):
                    src = (s + NS - t) % NS
                    remote(
                        red.at[lane, src], red.at[lane, src], ssem2.at[0, 0], rsem.at[lane, src], to_tensor(s)
                    ).wait_recv()
                    return 0

                lax.fori_loop(1, NS, wait, 0)
                red[lane, s] = part[lane * NS + s]
                total = red[lane, 0]
                for t in range(1, NS):
                    total = total + red[lane, t]
                res[lane * NS + s] = total.astype(BF16)

                def send(t, _):
                    to = (s + t) % NS
                    piece = res.at[lane * NS + s]
                    remote(piece, piece, ssem2.at[lane, t], rsem2.at[lane, s], to_tensor(to)).start()
                    return 0

                lax.fori_loop(1, NS, send, 0)
            if (lane + 1) * NS <= count:
                go()
            else:
                pl.when(s < count - lane * NS)(go)

    def gather_wait(res, count, ssem2, rsem2):
        def one(t, _):
            src = (s + NS - t) % NS
            for lane in range((count + NS - 1) // NS):
                def wait(lane=lane, src=src):
                    piece = res.at[lane * NS + src]
                    remote(piece, piece, ssem2.at[0, 0], rsem2.at[lane, src], to_tensor(s)).wait_recv()
                if (lane + 1) * NS <= count:
                    wait()
                else:
                    pl.when(src < count - lane * NS)(wait)
            return 0

        lax.fori_loop(1, NS, one, 0)

    def sent(part, res, count, ssem, ssem2):
        def one(t, _):
            to = (s + t) % NS
            for lane in range((count + NS - 1) // NS):
                def wait1(lane=lane, to=to):
                    piece = part.at[lane * NS + to]
                    remote(piece, piece, ssem.at[lane, t], ssem.at[lane, t], to_tensor(s)).wait_send()

                def wait2(lane=lane):
                    piece = res.at[lane * NS + s]
                    remote(piece, piece, ssem2.at[lane, t], ssem2.at[lane, t], to_tensor(s)).wait_send()
                if (lane + 1) * NS <= count:
                    wait1()
                    wait2()
                else:
                    pl.when(to < count - lane * NS)(wait1)
                    pl.when(s < count - lane * NS)(wait2)
            return 0

        lax.fori_loop(1, NS, one, 0)

    def spread(res, base):
        def body(qq, _):
            for n in range(NB):
                hit = jnp.int32(0)
                for o in range(OWN):
                    hit = hit + jnp.where(owned[qq * OWN + o] == ids_me[n], 1, 0)
                val = jnp.where(hit > 0, 1.0, 0.0).astype(F32)
                big[pl.ds(pl.multiple_of(qq * RK, RK), RK), n * RB : (n + 1) * RB] = (
                    res[base + n].astype(F32) * val
                ).astype(BF16)
            return 0

        lax.fori_loop(0, NQ, body, 0)

    def packet(res, base, right, out, lo, hi, scale):
        spread(res, base)
        d = jnp.dot(big[...], right, preferred_element_type=F32)
        if scale != 1.0:
            d = d * scale
        out[:, :, lo:hi] = d.astype(BF16).reshape(NQ, RK, hi - lo)

    def exchange(g, src, dst):
        def one(t, _):
            to = (q + t) % NQ
            remote(src.at[to], dst.at[q], a2s.at[g, t], a2r.at[g, q], to_dp(to)).start()
            return 0

        lax.fori_loop(1, NQ, one, 0)
        dst[q] = src[q]

    def exchanged(g, dst):
        def one(t, _):
            src = (q + NQ - t) % NQ
            remote(dst.at[src], dst.at[src], a2s.at[g, 0], a2r.at[g, src], to_dp(q)).wait_recv()
            return 0

        lax.fori_loop(1, NQ, one, 0)

    def exchange_sent(g, src):
        def one(t, _):
            to = (q + t) % NQ
            remote(src.at[to], src.at[to], a2s.at[g, t], a2r.at[g, 0], to_dp(q)).wait_send()
            return 0

        lax.fori_loop(1, NQ, one, 0)

    outs = []

    def put(src, dst):
        cp = pltpu.make_async_copy(src, dst, out_sem.at[len(outs)])
        cp.start()
        outs.append(cp)

    def collect(dst, lo, hi, stage, out):
        d = jnp.dot(pick[...], dst[:, :, lo:hi].reshape(NQ * RK, hi - lo), preferred_element_type=F32)
        stage[...] = d.reshape(OWN, RK, hi - lo)
        put(stage, out)

    unit = 4.93
    events = []
    for now, kind, u, v in weight_timeline(unit):
        if (u, v) != (0, 0):
            events.append((now, "w", (kind, u, v)))
    for d in range(1, 5):
        for h in range(2):
            for off in (-d, d):
                if d == 4 and (off < 0) != (h == 0):
                    continue
                when = 1.5 + unit * 12 / 7 * (2 * (d - 1) + (h if d < 4 else 0) + 1)
                events.append((when, "d", (off, h)))
    last_dy = max(e[0] for e in events if e[1] == "d")
    ready = {}
    for now, what, a in events:
        if what == "w":
            o = (a[1], a[2]) if a[0] < 2 else (a[2], a[1])
            ready[o] = max(ready.get(o, 0.0), now)
    ready[(0, 0)] = 0.0
    pieces = [(2.0, waits(2, 4))] + [(2.5 + 1.0 * n, lambda n=n: act(n)) for n in range(NB)]
    pieces += [(9.0, waits(0, 2)), (9.0, waits(4, 11))]
    pieces += [(12.0 + 4.0 * n, lambda n=n: ranks(n)) for n in range(NB)]
    pieces += [(40.0, picker)]

    def dy_done():
        for off in list(range(-3, 5)):
            for h in range(2):
                cwait(off, h)
        scatter(part1, red1, 4 * NB, rs1s, rs1r)

    pieces += [(last_dy + 1.5, dy_done)]
    at = last_dy + 1.6
    for i, (o, when) in enumerate(sorted(ready.items(), key=lambda kv: (kv[1], kv[0]))):
        at = max(at + 1.2, when + 0.1)
        pieces.append((at, lambda o=o, i=i: product(o[0], o[1], i == 0)))

    def reduce1():
        gather_sum(part1, red1, res1, 4 * NB, rs1r, ag1s, ag1r)

    def down_packets():
        gather_wait(res1, 4 * NB, ag1s, ag1r)
        packet(res1, 3 * NB, hid[...], s_d, 0, FW, SCALE)
        packet(res1, 2 * NB, dyf[s], s_d, FW, FW + WD, SCALE)
        exchange(0, s_d, r_d)
        for n in range(NB):
            acc[rows(n), :] = acc[rows(n), :] + SCALE * turned_dot(res1[3 * NB + n], tf[2, ids_me[n]])

    pieces += [(last_dy + 7.0, reduce1), (last_dy + 12.0, down_packets)]

    line = [(e[0], i, e[1], e[2]) for i, e in enumerate(events)]
    line += [(t, 1000 + i, "c", f) for i, (t, f) in enumerate(pieces)]
    for _, _, what, a in sorted(line, key=lambda e: (e[0], e[1])):
        if what == "w":
            wwait(*a)
            wforward(*a)
        elif what == "d":
            dwait(*a)
            dforward(*a)
        else:
            a()

    @pl.loop(0, acc.shape[0] // 16)
    def _(i):
        r = pl.ds(pl.multiple_of(i * 16, 16), 16)
        h = acc[r, :]
        gp[r, :] = (h * fa[r, :]).astype(BF16)
        up[r, :] = (h * fb[r, :]).astype(BF16)

    for n in range(NB):
        part2[n] = SCALE * rows_dot(tf[0, ids_me[n]], gp[rows(n), :])
        part2[NB + n] = SCALE * rows_dot(tf[1, ids_me[n]], up[rows(n), :])
    scatter(part2, red2, 2 * NB, rs2s, rs2r)
    packet(res1, 0, gp[...], s_o, 0, FW, SCALE)
    packet(res1, NB, up[...], s_o, FW, 2 * FW, SCALE)
    exchange(1, s_o, r_o)
    gather_sum(part2, red2, res2, 2 * NB, rs2r, ag2s, ag2r)
    exchanged(0, r_d)
    collect(r_d, 0, FW, st_f.at[0], o_din)
    collect(r_d, FW, FW + WD, st_w.at[0], o_dout)
    gather_wait(res2, 2 * NB, ag2s, ag2r)
    packet(res2, 0, xb[...], s_i, 0, WD, 1.0)
    packet(res2, NB, xb[...], s_i, WD, 2 * WD, 1.0)
    exchange(2, s_i, r_i)
    for n in range(NB):
        a = ids_me[n]
        d = turned_dot(res2[n], tw[0, a]) + turned_dot(res2[NB + n], tw[1, a])
        ig[rows(n), :] = d.astype(BF16)
    put(ig, ig_h)
    exchanged(1, r_o)
    collect(r_o, 0, FW, st_f.at[1], o_gout)
    collect(r_o, FW, 2 * FW, st_f.at[2], o_uout)
    exchanged(2, r_i)
    collect(r_i, 0, WD, st_w.at[1], o_gin)
    collect(r_i, WD, 2 * WD, st_w.at[2], o_uin)

    for i in range(wcount[0]):
        piece = wf.at[0, pl.ds(0, QR), :]
        remote(piece, piece, wsend.at[i], wrecv.at[0], to_dp(q)).wait_send()
    for i in range(dcount[0]):
        piece = dyf.at[0, pl.ds(0, HR), :]
        remote(piece, piece, dsend.at[i], drecv.at[0], to_tensor(s)).wait_send()
    for i in range(ccount[0]):
        piece = dyf.at[0, pl.ds(0, HR), :]
        remote(piece, piece, csend.at[i], crecv.at[0], to_tensor(s)).wait_send()
    sent(part1, res1, 4 * NB, rs1s, ag1s)
    sent(part2, res2, 2 * NB, rs2s, ag2s)
    exchange_sent(0, s_d)
    exchange_sent(1, s_o)
    exchange_sent(2, s_i)
    for cp in outs:
        cp.wait()


def shards(dy, xin, gpre, upre, w, gin, gout, uin, uout, din, dout, ids, owned):
    NQ, NS = lax.axis_size("dp"), lax.axis_size("tensor")
    T, WD = dy.shape
    FW = gpre.shape[1]
    A, RK = gin.shape[:2]
    NB = ids.shape[0] // NQ
    OWN = A // NQ
    RB = T // NB
    dims = (NB, RB, WD, FW, NQ, NS, OWN, RK)
    any_ = pl.BlockSpec(memory_space=pl.ANY)
    smem = pl.BlockSpec(memory_space=pltpu.SMEM)
    V = pltpu.VMEM
    D = pltpu.SemaphoreType.DMA
    outs = (
        jax.ShapeDtypeStruct((T, WD), BF16),
        jax.ShapeDtypeStruct((OWN, RK, WD), F32),
        jax.ShapeDtypeStruct((OWN, RK, FW), F32),
        jax.ShapeDtypeStruct((OWN, RK, WD), F32),
        jax.ShapeDtypeStruct((OWN, RK, FW), F32),
        jax.ShapeDtypeStruct((OWN, RK, FW), F32),
        jax.ShapeDtypeStruct((OWN, RK, WD), F32),
    )
    scratch = [
        V((NS, T, WD), BF16), V((NQ,) + w.shape, BF16), V((T, WD), BF16), V((T, FW), BF16), V((T, FW), BF16),
        V((3, A, RK, WD), BF16), V((3, A, RK, FW), BF16),
        V((T, FW), F32), V((T, FW), F32), V((T, FW), BF16), V((T, FW), F32),
        V((4 * NB, RK, RB), F32), V((2, NS, RK, RB), F32), V((4 * NB, RK, RB), BF16),
        V((2 * NB, RK, RB), F32), V((1, NS, RK, RB), F32), V((2 * NB, RK, RB), BF16),
        V((NQ * RK, T), BF16), V((OWN * RK, NQ * RK), BF16),
        V((NQ, RK, FW + WD), BF16), V((NQ, RK, 2 * FW), BF16), V((NQ, RK, 2 * WD), BF16),
        V((NQ, RK, FW + WD), BF16), V((NQ, RK, 2 * FW), BF16), V((NQ, RK, 2 * WD), BF16),
        V((T, WD), BF16), V((3, OWN, RK, WD), F32), V((3, OWN, RK, FW), F32),
        D((11,)), D((7,)), D((14,)), D((16,)), D((16,)), D((16,)), D((60,)), D((64,)),
        D((2, NS)), D((2, NS)), D((2, NS)), D((2, NS)), D((1, NS)), D((1, NS)), D((1, NS)), D((1, NS)),
        D((3, NQ)), D((3, NQ)),
    ]
    return pl.pallas_call(
        lambda *refs: kernel(dims, *refs),
        out_shape=outs,
        in_specs=[any_] * 11 + [smem] * 2,
        out_specs=tuple([any_] * 7),
        scratch_shapes=scratch,
        compiler_params=pltpu.CompilerParams(
            collective_id=0, has_side_effects=True, vmem_limit_bytes=67043328
        ),
        name="step",
    )(dy, xin, gpre, upre, w, gin, gout, uin, uout, din, dout, ids, owned)


def solution(mesh):
    wide = P("dp", "tensor")
    table = P(None, None, "tensor")
    owner = P("dp", None, "tensor")
    return jax.shard_map(
        shards,
        mesh=mesh,
        in_specs=(wide,) * 4 + (P("tensor", "dp"),) + (table,) * 6 + (P(), P()),
        out_specs=(wide,) + (owner,) * 6,
        check_vma=False,
    )
```

time: 331 us -> 139 us (0.42)
  the two profiles are of different devices: /device:TPU:1 before, /device:TPU:37 now
where the time goes in v1:
time: 139 us
  Pallas kernels  132 us (95%)
  local copies, waits for them, and re-layouts  6.1 us (4%)
    pallas_call x1, Pallas kernels, shards(): pl.pallas_call(lambda *refs: kernel(dims, *refs), out_shape=outs, in_spec...  132 us
    unnamed x19, local copies, waits for them, and re-layouts  6.1 us

profile of v1, /device:TPU:37, one launch (start us, length us, event | category | flops | bytes accessed | tf_op | source)
XLA Modules:
  0.0 139.1 jit_solution(12739055388625775660)
XLA Ops:
  0.6 132.3 %step.1 = (bf16[768,512]{1,0:T(8,128)(2,1)}, f32[3,16,512]{2,1,0:T(8,128)}, f32[3,16,896]{2,1,0:T(8,128)}, f32[3,16,512]{2,1,0:T(8,128)}, f32[3,16,896]{2,1,0:T(...) custom-call(bf16[768,512]{1,0:T(8,128)(2,1)} %refs_0_.1, bf16[768,512]{1,0:T(8,128)(2,1)} %refs_1_.1, ...), custom_call_target="tpu_custom_call" | custom-call | tf_op jit(solution)/shard_map/step/pallas_call | solution.py:529
  133.0 0.0 copy-start.5
  133.0 0.0 copy-start.2
  133.0 0.0 copy-start.4
  133.0 0.0 copy-start.1
  133.0 0.0 copy-start
  133.0 0.0 copy-start.3
  133.0 2.1 %copy.27 = bf16[768,512]{1,0:T(8,128)(2,1)} copy(bf16[768,512]{1,0:T(8,128)(2,1)} %get-tuple-element.14) | data formatting | bytes 1572864
  135.2 0.0 copy-done.5
  135.2 0.6 copy.28
  135.8 0.0 copy-done.2
  135.8 0.7 copy.29
  136.5 0.0 copy-done.4
  136.5 0.6 copy.30
  137.1 0.0 copy-done.1
  137.2 0.7 copy.31
  137.8 0.0 copy-done
  137.8 0.7 copy.32
  138.5 0.0 copy-done.3
  138.5 0.6 copy.33
Async XLA Ops:
  133.0 2.2 %copy-start.5 = (f32[3,16,512]{2,1,0:T(8,128)S(1)}, f32[3,16,512]{2,1,0:T(8,128)}, u32[]{:S(2)}) copy-start(f32[3,16,512]{2,1,0:T(8,128)} %get-tuple-element.15) | copy-start | bytes 294916
  133.0 2.8 %copy-start.2 = (f32[3,16,896]{2,1,0:T(8,128)S(1)}, f32[3,16,896]{2,1,0:T(8,128)}, u32[]{:S(2)}) copy-start(f32[3,16,896]{2,1,0:T(8,128)} %get-tuple-element.16) | copy-start | bytes 516100
  133.0 3.5 %copy-start.4 = (f32[3,16,512]{2,1,0:T(8,128)S(1)}, f32[3,16,512]{2,1,0:T(8,128)}, u32[]{:S(2)}) copy-start(f32[3,16,512]{2,1,0:T(8,128)} %get-tuple-element.17) | copy-start | bytes 294916
  133.0 4.1 %copy-start.1 = (f32[3,16,896]{2,1,0:T(8,128)S(1)}, f32[3,16,896]{2,1,0:T(8,128)}, u32[]{:S(2)}) copy-start(f32[3,16,896]{2,1,0:T(8,128)} %get-tuple-element.18) | copy-start | bytes 516100
  133.0 4.8 %copy-start = (f32[3,16,896]{2,1,0:T(8,128)S(1)}, f32[3,16,896]{2,1,0:T(8,128)}, u32[]{:S(2)}) copy-start(f32[3,16,896]{2,1,0:T(8,128)} %get-tuple-element.19) | copy-start | bytes 516100
  133.0 5.5 %copy-start.3 = (f32[3,16,512]{2,1,0:T(8,128)S(1)}, f32[3,16,512]{2,1,0:T(8,128)}, u32[]{:S(2)}) copy-start(f32[3,16,512]{2,1,0:T(8,128)} %get-tuple-element.20) | copy-start | bytes 294916

commit v2 on v1

v2 whole, which is shorter than its diff:
```python
import heapq

import jax
import jax.numpy as jnp
from jax import lax
from jax.experimental import pallas as pl
from jax.experimental.pallas import tpu as pltpu
from jax.sharding import PartitionSpec as P

SCALE = 2.0
F32 = jnp.float32
BF16 = jnp.bfloat16
MESH = pl.DeviceIdType.MESH
RING = 4
DEPTH = 8


def centred(a):
    return ((a + 1) % RING) - 1


def weight_hops(kind, u, v):
    sign = 1 if kind % 2 == 0 else -1
    first, second = ("x", "y") if kind < 2 else ("y", "x")
    hops = []
    if v == 0:
        if u == 0:
            hops += [(first, sign), (first, -sign)]
        elif u == -sign:
            hops += [(first, sign)]
        hops += [(second, sign), (second, -sign)]
    elif v == -sign:
        hops += [(second, sign)]
    return first, hops


def weight_timeline(unit):
    free = {(a, s): 0.0 for a in "xy" for s in (1, -1)}
    order, count = [], 0
    heap = [(0.0, k - 4, k, 0, 0) for k in range(4)]
    heapq.heapify(heap)
    while heap:
        now, _, kind, u, v = heapq.heappop(heap)
        order.append((now, kind, u, v))
        first, hops = weight_hops(kind, u, v)
        for axis, sign in hops:
            end = max(free[(axis, sign)], now) + unit
            free[(axis, sign)] = end
            nu, nv = (centred(u - sign), v) if axis == first else (u, centred(v - sign))
            heapq.heappush(heap, (end + 1.5, count, kind, nu, nv))
            count += 1
    return order


def rows_dot(a, b):
    return lax.dot_general(a, b, (((1,), (1,)), ((), ())), preferred_element_type=F32)


def turned_dot(a, b):
    return jnp.dot(a.astype(F32).T.astype(BF16), b, preferred_element_type=F32)


def kernel(
    dims,
    dy_h, x_h, gp_h, up_h, w_h, gin_h, gout_h, uin_h, uout_h, din_h, dout_h, ids, owned,
    ig_h, o_gout, o_uout, o_din, o_dout, r_i, pick_h,
    dyf, wf, xb, gp, up, tw, tf, fa, fb, hid, acc, part1, red1, res1, part2, red2, res2, big, mask, pick,
    s_d, s_o, s_i, r_d, r_o, ig, st_w, st_f,
    loc_sem, out_sem, dsend, drecv, csend, crecv, wsend, wrecv,
    rs1s, rs1r, ag1s, ag1r, rs2s, rs2r, ag2s, ag2r, a2s, a2r,
):
    NB, RB, WD, FW, NQ, NS, OWN, RK = dims
    q = lax.axis_index("dp")
    s = lax.axis_index("tensor")
    x, y = q // RING, q % RING
    z, c = s // 2, s % 2

    def dp_at(axis, sign):
        if axis == "x":
            return ((x + sign + RING) % RING) * RING + y
        return x * RING + (y + sign + RING) % RING

    def to_dp(qq):
        return {"dp": qq, "tensor": s}

    def to_tensor(ss):
        return {"dp": q, "tensor": ss}

    def z_at(off):
        return (z + off + DEPTH) % DEPTH

    def remote(src, dst, ss, rs, dev):
        return pltpu.make_async_remote_copy(
            src_ref=src, dst_ref=dst, send_sem=ss, recv_sem=rs, device_id=dev, device_id_type=MESH
        )

    loads = [
        (gp_h, gp), (up_h, up), (dy_h, dyf.at[s]), (x_h, xb), (w_h, wf.at[q]),
        (gin_h, tw.at[0]), (uin_h, tw.at[1]), (dout_h, tw.at[2]),
        (gout_h, tf.at[0]), (uout_h, tf.at[1]), (din_h, tf.at[2]),
    ]
    loads = [pltpu.make_async_copy(a, b, loc_sem.at[i]) for i, (a, b) in enumerate(loads)]

    barrier = pltpu.get_barrier_semaphore()
    peers = [to_dp(dp_at(a, sg)) for a in "xy" for sg in (1, -1)]
    peers += [to_tensor(z_at(1) * 2 + c), to_tensor(z_at(-1) * 2 + c), to_tensor(z * 2 + 1 - c)]
    for peer in peers:
        pl.semaphore_signal(barrier, inc=1, device_id=peer, device_id_type=MESH)
    pl.semaphore_wait(barrier, len(peers))

    QR = wf.shape[1] // 4
    wcount = [0]

    def wpiece(kind, u, v):
        ox, oy = (u, v) if kind < 2 else (v, u)
        qq = ((x + ox + RING) % RING) * RING + (y + oy + RING) % RING
        return wf.at[qq, pl.ds(kind * QR, QR), :]

    def wsem(kind, u, v):
        return kind * 16 + (u % RING) * RING + v % RING

    def wforward(kind, u, v):
        first, hops = weight_hops(kind, u, v)
        piece = wpiece(kind, u, v)
        src = w_h.at[pl.ds(kind * QR, QR), :] if (u, v) == (0, 0) else piece
        for axis, sign in hops:
            nu, nv = (centred(u - sign), v) if axis == first else (u, centred(v - sign))
            remote(
                src, piece, wsend, wrecv.at[wsem(kind, nu, nv)], to_dp(dp_at(axis, sign))
            ).start()
            wcount[0] += 1

    def wwait(kind, u, v):
        piece = wpiece(kind, u, v)
        remote(piece, piece, wsend, wrecv.at[wsem(kind, u, v)], to_dp(q)).wait_recv()

    HR = dyf.shape[1] // 4
    dcount = [0]
    ccount = [0]

    def dpiece(off, j, core):
        return dyf.at[z_at(off) * 2 + core, pl.ds(j * HR, HR), :]

    def dsem(off, j):
        return (off % DEPTH) * 4 + j

    def dsend_one(off, j, sign):
        piece = dpiece(off, j, c)
        src = dy_h.at[pl.ds(j * HR, HR), :] if off == 0 else piece
        remote(
            src, piece, dsend, drecv.at[dsem(off - sign, j)], to_tensor(z_at(sign) * 2 + c)
        ).start()
        dcount[0] += 1

    def dshare(off, j):
        piece = dpiece(off, j, c)
        src = dy_h.at[pl.ds(j * HR, HR), :] if off == 0 else piece
        remote(
            src, piece, csend, crecv.at[j // 2], to_tensor(z * 2 + 1 - c)
        ).start()
        ccount[0] += 1

    lane = [(0, 0), (0, 1), (0, 2), (1, 0), (1, 1), (0, 3), (2, 0), (2, 1), (1, 2), (3, 0), (1, 3), (2, 2), (2, 3), (3, 2)]
    waiting = {sign: [(-sign * d, j if sign > 0 else j ^ 1) for d, j in lane] for sign in (1, -1)}
    held = {(0, j) for j in range(4)}

    def dflush():
        for sign in (1, -1):
            while waiting[sign] and waiting[sign][0] in held:
                dsend_one(*waiting[sign].pop(0), sign)

    def dforward(off, j):
        held.add((off, j))
        dflush()
        dshare(off, j)

    def dwait(off, j):
        piece = dpiece(off, j, c)
        remote(piece, piece, dsend, drecv.at[dsem(off, j)], to_tensor(s)).wait_recv()

    def cwait():
        both = dyf.at[pl.ds(0, DEPTH // 2)]
        return lambda p: remote(both, both, csend, crecv.at[p], to_tensor(s)).wait_recv()

    for kind in range(4):
        wforward(kind, 0, 0)
    dflush()
    for j in range(4):
        dshare(0, j)
    for cp in loads:
        cp.start()

    outs = []

    def put(src, dst):
        cp = pltpu.make_async_copy(src, dst, out_sem.at[len(outs)])
        cp.start()
        outs.append(cp)

    ids_me = [ids[q * NB + n] for n in range(NB)]

    def rows(n):
        return pl.ds(n * RB, RB)

    def act(n):
        @pl.loop(0, RB // 16)
        def _(i):
            r = pl.ds(pl.multiple_of(n * RB + i * 16, 16), 16)
            g = gp[r, :].astype(F32)
            u = up[r, :].astype(F32)
            sg = jax.nn.sigmoid(g)
            b = g * sg
            fb[r, :] = b
            fa[r, :] = u * sg * (1.0 + g * (1.0 - sg))
            hid[r, :] = (b * u).astype(BF16)

    def ranks(n):
        a = ids_me[n]
        slab(part1, n)[...] = rows_dot(tw[0, a], xb[rows(n), :])
        slab(part1, NB + n)[...] = rows_dot(tw[1, a], xb[rows(n), :])
        slab(part1, 2 * NB + n)[...] = rows_dot(tf[2, a], hid[rows(n), :])
        slab(part1, 3 * NB + n)[...] = rows_dot(tw[2, a], dyf[s, rows(n), :])

    def picker():
        row = lax.broadcasted_iota(jnp.int32, (OWN * RK, NQ * RK), 0)
        col = lax.broadcasted_iota(jnp.int32, (OWN * RK, NQ * RK), 1)
        same = (row % RK) == (col % RK)
        rown, cown = row // RK, col // RK

        def body(qq, m):
            for o in range(OWN):
                mine = owned[q * OWN + o]
                hit = jnp.int32(0)
                for n in range(NB):
                    hit = hit + jnp.where(ids[qq * NB + n] == mine, 1, 0)
                val = jnp.where(hit > 0, 1.0, 0.0).astype(F32)
                m = m + jnp.where((cown == qq) & (rown == o) & same, 1.0, 0.0) * val
            return m

        pick[...] = lax.fori_loop(0, NQ, body, jnp.zeros((OWN * RK, NQ * RK), F32)).astype(BF16)
        put(pick, pick_h)

    def waits(a, b):
        def run():
            for cp in loads[a:b]:
                cp.wait()

        return run

    half_rows = acc.shape[0] // 2

    def product(ox, oy, half, fresh=False):
        if isinstance(oy, tuple):
            oy = oy[0] + (y + oy[0] + c + oy[2]) % 2 * oy[1]
        k = ((x + ox + RING) % RING) * RING + (y + oy + RING) % RING
        r = slice(half * half_rows, (half + 1) * half_rows)
        d = rows_dot(dyf[k, r, :], wf[k])
        acc[r, :] = d if fresh else acc[r, :] + d

    def scatter(part, red, ssem, rsem):
        def one(t, _):
            to = (s + t) % NS

            @pl.when(to < part.shape[0])
            def _():
                remote(part.at[to], red.at[s], ssem, rsem, to_tensor(to)).start()

            return 0

        lax.fori_loop(1, NS, one, 0)

    def gather_sum(part, red, res, rsem, ssem2, rsem2):
        @pl.when(s < part.shape[0])
        def _():
            others_ = red.at[pl.ds(0, NS - 1)]
            remote(others_, others_, ssem2.at[0], rsem, to_tensor(s)).wait_recv()
            red[s] = part[s]
            total = red[0]
            for t in range(1, NS):
                total = total + red[t]
            res[s] = total.astype(BF16)

            def send(t, _):
                to = (s + t) % NS
                remote(res.at[s], res.at[s], ssem2.at[t], rsem2, to_tensor(to)).start()
                return 0

            lax.fori_loop(1, NS, send, 0)

    def each_way(ref, go):
        many = ref.shape[0]
        pl.when(s < many)(lambda: go(ref.at[pl.ds(0, many - 1)]))
        pl.when(s >= many)(lambda: go(ref))

    def gather_wait(res, ssem2, rsem2):
        each_way(res, lambda r: remote(r, r, ssem2.at[0], rsem2, to_tensor(s)).wait_recv())

    def sent(part, res, ssem, ssem2):
        each_way(part, lambda r: remote(r, r, ssem, ssem, to_tensor(s)).wait_send())

        @pl.when(s < res.shape[0])
        def _():
            def one(t, _):
                remote(res.at[s], res.at[s], ssem2.at[t], ssem2.at[t], to_tensor(s)).wait_send()
                return 0

            lax.fori_loop(1, NS, one, 0)

    def slab(ref, i):
        per = ref.shape[1] // RK
        return ref.at[i // per, pl.ds(i % per * RK, RK), :]

    def masks():
        def body(qq, _):
            for n in range(NB):
                hit = jnp.int32(0)
                for o in range(OWN):
                    hit = hit + jnp.where(owned[qq * OWN + o] == ids_me[n], 1, 0)
                val = jnp.where(hit > 0, 1.0, 0.0).astype(F32)
                mask[pl.ds(pl.multiple_of(qq * RK, RK), RK), n * RB : (n + 1) * RB] = jnp.full((RK, RB), val).astype(BF16)
            return 0

        lax.fori_loop(0, NQ, body, 0)

    def spread(res, base):
        row = jnp.concatenate([slab(res, base + n)[...] for n in range(NB)], axis=1)
        for qq in range(NQ):
            big[qq * RK : (qq + 1) * RK, :] = row * mask[qq * RK : (qq + 1) * RK, :]

    def packet(res, base, right, out, lo, hi, scale):
        spread(res, base)
        d = jnp.dot(big[...], right, preferred_element_type=F32)
        if scale != 1.0:
            d = d * scale
        out[:, :, lo:hi] = d.astype(BF16).reshape(NQ, RK, hi - lo)

    ring = (2, 1, -1, 0)
    others = [(a, b) for a in ring for b in ring if (a, b) != (0, 0)]
    others.sort(key=lambda o: -(abs(o[0]) + abs(o[1])))

    def peer(o, sign=1):
        return ((x + sign * o[0] + RING) % RING) * RING + (y + sign * o[1] + RING) % RING

    def exchange(g, src, dst):
        for o in others:
            to = peer(o)
            remote(src.at[to], dst.at[q], a2s.at[g], a2r.at[g], to_dp(to)).start()

    def exchanged(g, dst):
        all_ = dst.at[pl.ds(0, NQ - 1)]
        remote(all_, all_, a2s.at[g], a2r.at[g], to_dp(q)).wait_recv()

    def exchange_sent(g, src):
        all_ = src.at[pl.ds(0, NQ - 1)]
        remote(all_, all_, a2s.at[g], a2r.at[g], to_dp(q)).wait_send()

    def collect(dst, lo, hi, stage, out):
        d = jnp.dot(pick[...], dst[:, :, lo:hi].reshape(NQ * RK, hi - lo), preferred_element_type=F32)
        stage[...] = d.reshape(OWN, RK, hi - lo)
        put(stage, out)

    unit = 4.93
    events = []
    for now, kind, u, v in weight_timeline(unit):
        if (u, v) != (0, 0):
            events.append((now, "w", (kind, u, v)))
    quarter = unit * 12 / 14
    for i, (d, j) in enumerate(lane):
        for sign in (1, -1):
            events.append((3.5 + quarter * (i + 1) + (3.0 if i >= 11 else 0.0), "d", (-sign * (d + 1), j if sign > 0 else j ^ 1)))
    passed = [max(e[0] for e in events if e[1] == "d" and e[2][1] // 2 == p) for p in range(2)]
    ready = {}
    for now, what, a in events:
        if what == "w":
            o = (a[1], a[2]) if a[0] < 2 else (a[2], a[1])
            ready[o] = max(ready.get(o, 0.0), now)
    last_hop = max(e[0] for e in events if e[1] == "w" and len(weight_hops(*e[2])[1]) > 0)
    ready[(0, 0)] = 0.0

    pass_done = cwait()

    def start_ranks():
        scatter(part1, red1, rs1s, rs1r)

    def reduce1():
        gather_sum(part1, red1, res1, rs1r, ag1s, ag1r)

    def down_packets():
        gather_wait(res1, ag1s, ag1r)
        packet(res1, 3 * NB, hid[...], s_d, 0, FW, SCALE)
        packet(res1, 2 * NB, dyf[s], s_d, FW, FW + WD, SCALE)
        r_d[q] = s_d[q]

    def down_out():
        exchange(0, s_d, r_d)

    def adapter_term(n):
        acc[rows(n), :] = acc[rows(n), :] + SCALE * turned_dot(slab(res1, 3 * NB + n)[...], tf[2, ids_me[n]])

    pieces = [(2.0, waits(0, 2))] + [(2.5 + 1.0 * n, lambda n=n: act(n)) for n in range(NB)]
    pieces += [(9.0, waits(2, 11))]
    pieces += [(11.0 + 3.0 * n, lambda n=n: ranks(n)) for n in range(NB)]
    pieces += [(29.5, picker), (32.0, masks)]
    begun = (passed[0] + 5.0, passed[1] + 3.0)
    pieces += [(begun[p], lambda p=p: pass_done(p)) for p in range(2)]
    pieces += [(begun[0] + 0.1, start_ranks), (passed[1] + 0.1, reduce1)]
    pieces += [(last_hop + 1.4, down_packets), (last_hop + 1.5, down_out)]
    by_time = [o for o, _ in sorted(ready.items(), key=lambda kv: (kv[1], kv[0]))]
    first = [(ox, (0, 1, 0)) for ox in (0, -1, 1, 2)] + [(0, (2, -3, 0))]
    second = [(ox, (0, 1, 1)) for ox in (0, -1, 1, 2)] + [(0, (2, -3, 1))]
    paired = [(ox, oy) for ox in (0, -1, 1, 2) for oy in (0, 1)] + [(0, 2), (0, -1)]
    orders = [by_time, first + second + [o for o in by_time if o not in paired]]
    for half in range(2):
        at = (begun[0], passed[1])[half] + 0.2
        for i, o in enumerate(orders[half]):
            at = max(at + 0.5, ready.get(o, 0.0) + 0.1)
            if half == 1 and i == len(first):
                at = max(at, begun[1] + 0.1)
            pieces.append((at, lambda o=o, i=i, half=half: product(o[0], o[1], half, i == 0)))
    pieces += [(last_hop + 1.6 + 0.1 * n, lambda n=n: adapter_term(n)) for n in range(NB)]

    line = [(e[0], i, e[1], e[2]) for i, e in enumerate(events)]
    line += [(t, 1000 + i, "c", f) for i, (t, f) in enumerate(pieces)]
    for _, _, what, a in sorted(line, key=lambda e: (e[0], e[1])):
        if what == "w":
            wwait(*a)
            wforward(*a)
        elif what == "d":
            dwait(*a)
            dforward(*a)
        else:
            a()

    @pl.loop(0, acc.shape[0] // 16)
    def _(i):
        r = pl.ds(pl.multiple_of(i * 16, 16), 16)
        h = acc[r, :]
        gp[r, :] = (h * fa[r, :]).astype(BF16)
        up[r, :] = (h * fb[r, :]).astype(BF16)

    for n in range(NB):
        part2[n] = SCALE * rows_dot(tf[0, ids_me[n]], gp[rows(n), :])
        part2[NB + n] = SCALE * rows_dot(tf[1, ids_me[n]], up[rows(n), :])
    scatter(part2, red2, rs2s, rs2r)
    packet(res1, 0, gp[...], s_o, 0, FW, SCALE)
    packet(res1, NB, up[...], s_o, FW, 2 * FW, SCALE)
    exchange(1, s_o, r_o)
    r_o[q] = s_o[q]
    gather_sum(part2, red2, res2, rs2r, ag2s, ag2r)
    exchanged(0, r_d)
    collect(r_d, 0, FW, st_f.at[0], o_din)
    collect(r_d, FW, FW + WD, st_w, o_dout)
    gather_wait(res2, ag2s, ag2r)
    packet(res2, 0, xb[...], s_i, 0, WD, 1.0)
    packet(res2, NB, xb[...], s_i, WD, 2 * WD, 1.0)
    exchange(2, s_i, r_i)
    put(s_i.at[q], r_i.at[q])
    for n in range(NB):
        a = ids_me[n]
        d = turned_dot(res2[n], tw[0, a]) + turned_dot(res2[NB + n], tw[1, a])
        ig[rows(n), :] = d.astype(BF16)
    put(ig, ig_h)
    exchanged(1, r_o)
    collect(r_o, 0, FW, st_f.at[1], o_gout)
    collect(r_o, FW, 2 * FW, st_f.at[2], o_uout)
    exchanged(2, r_i)

    assert wcount[0] % 4 == dcount[0] % 4 == ccount[0] % 4 == 0
    for ref, many, ss, rs in ((wf, wcount, wsend, wrecv.at[0]), (dyf, dcount, dsend, drecv.at[0]), (dyf, ccount, csend, crecv.at[0])):
        whole = ref.at[pl.ds(0, many[0] // 4)]
        remote(whole, whole, ss, rs, to_dp(q)).wait_send()
    sent(part1, res1, rs1s, ag1s)
    sent(part2, res2, rs2s, ag2s)
    exchange_sent(0, s_d)
    exchange_sent(1, s_o)
    exchange_sent(2, s_i)
    for cp in outs:
        cp.wait()


def shards(dy, xin, gpre, upre, w, gin, gout, uin, uout, din, dout, ids, owned):
    NQ, NS = lax.axis_size("dp"), lax.axis_size("tensor")
    T, WD = dy.shape
    FW = gpre.shape[1]
    A, RK = gin.shape[:2]
    NB = ids.shape[0] // NQ
    OWN = A // NQ
    RB = T // NB
    dims = (NB, RB, WD, FW, NQ, NS, OWN, RK)
    any_ = pl.BlockSpec(memory_space=pl.ANY)
    smem = pl.BlockSpec(memory_space=pltpu.SMEM)
    V = pltpu.VMEM
    D = pltpu.SemaphoreType.DMA
    wide, tall = jax.ShapeDtypeStruct((OWN, RK, WD), F32), jax.ShapeDtypeStruct((OWN, RK, FW), F32)
    flat = jax.ShapeDtypeStruct((T, WD), BF16)
    outs = (
        flat, tall, tall, tall, wide,
        jax.ShapeDtypeStruct((NQ, RK, 2 * WD), BF16), jax.ShapeDtypeStruct((OWN * RK, NQ * RK), BF16),
    )
    scratch = [
        V((NS, T, WD), BF16), V((NQ,) + w.shape, BF16), V((T, WD), BF16), V((T, FW), BF16), V((T, FW), BF16),
        V((3, A, RK, WD), BF16), V((3, A, RK, FW), BF16),
        V((T, FW), F32), V((T, FW), F32), V((T, FW), BF16), V((T, FW), F32),
        V((2 * NB, 2 * RK, RB), F32), V((NS, 2 * RK, RB), F32), V((2 * NB, 2 * RK, RB), BF16),
        V((2 * NB, RK, RB), F32), V((NS, RK, RB), F32), V((2 * NB, RK, RB), BF16),
        V((NQ * RK, T), BF16), V((NQ * RK, T), BF16), V((OWN * RK, NQ * RK), BF16),
        V((NQ, RK, FW + WD), BF16), V((NQ, RK, 2 * FW), BF16), V((NQ, RK, 2 * WD), BF16),
        V((NQ, RK, FW + WD), BF16), V((NQ, RK, 2 * FW), BF16),
        V((T, WD), BF16), V((OWN, RK, WD), F32), V((3, OWN, RK, FW), F32),
        D((11,)), D((7,)), D, D((32,)), D, D((2,)), D, D((64,)), D, D, D((NS,)), D, D, D, D((NS,)), D, D((3,)), D((3,)),
    ]
    ig, gate_out, up_out, down_in, down_out, late, pick = pl.pallas_call(
        lambda *refs: kernel(dims, *refs),
        out_shape=outs,
        in_specs=[any_] * 11 + [smem] * 2,
        out_specs=tuple([any_] * 7),
        scratch_shapes=scratch,
        compiler_params=pltpu.CompilerParams(
            collective_id=0, has_side_effects=True, vmem_limit_bytes=67043328
        ),
        name="step",
    )(dy, xin, gpre, upre, w, gin, gout, uin, uout, din, dout, ids, owned)
    return pl.pallas_call(
        finish,
        out_shape=(flat, wide, tall, wide, tall, tall, wide),
        in_specs=[any_] * 7,
        out_specs=tuple([any_] * 7),
        scratch_shapes=[
            V((NQ, RK, 2 * WD), BF16), V((OWN * RK, NQ * RK), BF16),
            V((T, WD), BF16), V((3, OWN, RK, FW), F32), V((3, OWN, RK, WD), F32), D((7,)), D((7,)),
        ],
        compiler_params=pltpu.CompilerParams(vmem_limit_bytes=67043328),
        name="finish",
    )(ig, gate_out, up_out, down_in, down_out, late, pick)


def finish(
    ig_i, gout_i, uout_i, din_i, dout_i, late_i, pick_i, ig_o, gin_o, gout_o, uin_o, uout_o, din_o, dout_o,
    late, pick, ig, tall, wide, in_sem, out_sem,
):
    RK, WD = wide.shape[2:]
    loads = [(late_i, late), (pick_i, pick), (ig_i, ig)]
    loads += [(gout_i, tall.at[0]), (uout_i, tall.at[1]), (din_i, tall.at[2]), (dout_i, wide.at[0])]
    loads = [pltpu.make_async_copy(a, b, in_sem.at[i]) for i, (a, b) in enumerate(loads)]
    for cp in loads:
        cp.start()
    stores = [(wide.at[1], gin_o), (wide.at[2], uin_o), (ig, ig_o)]
    stores += [(tall.at[0], gout_o), (tall.at[1], uout_o), (tall.at[2], din_o), (wide.at[0], dout_o)]
    stores = [pltpu.make_async_copy(a, b, out_sem.at[i]) for i, (a, b) in enumerate(stores)]
    for i in range(2):
        loads[i].wait()
    d = jnp.dot(pick[...], late[...].reshape(-1, 2 * WD), preferred_element_type=F32)
    wide[1] = d[:, :WD].reshape(-1, RK, WD)
    wide[2] = d[:, WD:].reshape(-1, RK, WD)
    for i in range(2):
        stores[i].start()
    for i in range(2, 7):
        loads[i].wait()
        stores[i].start()
    for cp in stores:
        cp.wait()


def solution(mesh):
    wide = P("dp", "tensor")
    table = P(None, None, "tensor")
    owner = P("dp", None, "tensor")
    return jax.shard_map(
        shards,
        mesh=mesh,
        in_specs=(wide,) * 4 + (P("tensor", "dp"),) + (table,) * 6 + (P(), P()),
        out_specs=(wide,) + (owner,) * 6,
        check_vma=False,
    )
```

time: 139 us -> 119 us (0.86)
  the two profiles are of different devices: /device:TPU:37 before, /device:TPU:1 now
where the time goes in v2:
time: 119 us; the launch traced here: 118 us
  Pallas kernels  117 us (98%)
    pallas_call x1, Pallas kernels, shards(): pl.pallas_call(lambda *refs: kernel(dims, *refs), out_shape=outs, in_spec...  115 us
    pallas_call x1, Pallas kernels, shards(): pl.pallas_call(finish, out_shape=(flat, wide, tall, wide, tall, tall, wid...  2.51 us

profile of v2, /device:TPU:1, one launch (start us, length us, event | category | flops | bytes accessed | tf_op | source)
XLA Modules:
  0.0 118.1 jit_solution(5208080353419612892)
XLA Ops:
  0.6 114.8 %step.1 = (bf16[768,512]{1,0:T(8,128)(2,1)}, f32[3,16,896]{2,1,0:T(8,128)}, f32[3,16,896]{2,1,0:T(8,128)}, f32[3,16,896]{2,1,0:T(8,128)}, f32[3,16,512]{2,1,0:T(...) custom-call(bf16[768,512]{1,0:T(8,128)(2,1)} %refs_0_.1, bf16[768,512]{1,0:T(8,128)(2,1)} %refs_1_.1, ...), custom_call_target="tpu_custom_call" | custom-call | tf_op jit(solution)/shard_map/step/pallas_call | solution.py:512
  115.5 2.5 %finish.1 = (bf16[768,512]{1,0:T(8,128)(2,1)}, f32[3,16,512]{2,1,0:T(8,128)}, f32[3,16,896]{2,1,0:T(8,128)}, f32[3,16,512]{2,1,0:T(8,128)}, f32[3,16,896]{2,1,0:...) custom-call(bf16[768,512]{1,0:T(8,128)(2,1)} %get-tuple-element.14.ig_i, f32[3,16,896]{2,1,0:T(8,128)} %get-tuple-element.15.gout_i, ...), custom_call_target="tpu_custom_call" | custom-call | tf_op jit(solution)/shard_map/finish/pallas_call | solution.py:523

commit v3 on v2

--- a/solution.py
+++ b/solution.py
@@ -101,6 +101,9 @@
     ]
     loads = [pltpu.make_async_copy(a, b, loc_sem.at[i]) for i, (a, b) in enumerate(loads)]
 
+    for cp in loads[:2]:
+        cp.start()
+
     barrier = pltpu.get_barrier_semaphore()
     peers = [to_dp(dp_at(a, sg)) for a in "xy" for sg in (1, -1)]
     peers += [to_tensor(z_at(1) * 2 + c), to_tensor(z_at(-1) * 2 + c), to_tensor(z * 2 + 1 - c)]
@@ -156,7 +159,7 @@
         piece = dpiece(off, j, c)
         src = dy_h.at[pl.ds(j * HR, HR), :] if off == 0 else piece
         remote(
-            src, piece, csend, crecv.at[j // 2], to_tensor(z * 2 + 1 - c)
+            src, piece, csend, crecv.at[0 if j < 2 else 1 if abs(off) < 3 else 2], to_tensor(z * 2 + 1 - c)
         ).start()
         ccount[0] += 1
 
@@ -178,16 +181,16 @@
         piece = dpiece(off, j, c)
         remote(piece, piece, dsend, drecv.at[dsem(off, j)], to_tensor(s)).wait_recv()
 
-    def cwait():
-        both = dyf.at[pl.ds(0, DEPTH // 2)]
-        return lambda p: remote(both, both, csend, crecv.at[p], to_tensor(s)).wait_recv()
+    def cwait(p):
+        both = dyf.at[pl.ds(0, (DEPTH, 5, DEPTH - 5)[p]), pl.ds(0, 2 * HR)]
+        remote(both, both, csend, crecv.at[p], to_tensor(s)).wait_recv()
 
     for kind in range(4):
         wforward(kind, 0, 0)
     dflush()
     for j in range(4):
         dshare(0, j)
-    for cp in loads:
+    for cp in loads[2:]:
         cp.start()
 
     outs = []
@@ -216,10 +219,10 @@
 
     def ranks(n):
         a = ids_me[n]
-        slab(part1, n)[...] = rows_dot(tw[0, a], xb[rows(n), :])
-        slab(part1, NB + n)[...] = rows_dot(tw[1, a], xb[rows(n), :])
-        slab(part1, 2 * NB + n)[...] = rows_dot(tf[2, a], hid[rows(n), :])
-        slab(part1, 3 * NB + n)[...] = rows_dot(tw[2, a], dyf[s, rows(n), :])
+        slab(part1, n)[...] = rows_dot(tw[0, a], xb[rows(n), :]).astype(BF16)
+        slab(part1, NB + n)[...] = rows_dot(tw[1, a], xb[rows(n), :]).astype(BF16)
+        slab(part1, 2 * NB + n)[...] = rows_dot(tf[2, a], hid[rows(n), :]).astype(BF16)
+        slab(part1, 3 * NB + n)[...] = rows_dot(tw[2, a], dyf[s, rows(n), :]).astype(BF16)
 
     def picker():
         row = lax.broadcasted_iota(jnp.int32, (OWN * RK, NQ * RK), 0)
@@ -249,13 +252,31 @@
 
     half_rows = acc.shape[0] // 2
 
-    def product(ox, oy, half, fresh=False):
-        if isinstance(oy, tuple):
-            oy = oy[0] + (y + oy[0] + c + oy[2]) % 2 * oy[1]
-        k = ((x + ox + RING) % RING) * RING + (y + oy + RING) % RING
+    def multiply(k, half, fresh=False):
         r = slice(half * half_rows, (half + 1) * half_rows)
         d = rows_dot(dyf[k, r, :], wf[k])
         acc[r, :] = d if fresh else acc[r, :] + d
+
+    def piece_at(ox, oy):
+        return ((x + ox + RING) % RING) * RING + (y + oy + RING) % RING
+
+    def near(k):
+        return (k // 2 + DEPTH + 2 - z) % DEPTH < 5
+
+    def soon(k):
+        ox, oy = (k // RING + RING - x) % RING, (k % RING + RING - y) % RING
+        return ((ox != 2) & (oy != 2)) | (ox + oy == 2) & (ox * oy == 0)
+
+    def early(dz, core):
+        k = z_at(dz) * 2 + core
+        pl.when(soon(k))(lambda: multiply(k, 1))
+
+    def late(ox, oy):
+        k = piece_at(ox, oy)
+        if abs(ox * oy) > 1:
+            multiply(k, 1)
+        else:
+            pl.when(jnp.logical_not(near(k)))(lambda: multiply(k, 1))
 
     def scatter(part, red, ssem, rsem):
         def one(t, _):
@@ -273,16 +294,16 @@
         @pl.when(s < part.shape[0])
         def _():
             others_ = red.at[pl.ds(0, NS - 1)]
-            remote(others_, others_, ssem2.at[0], rsem, to_tensor(s)).wait_recv()
+            remote(others_, others_, ssem2, rsem, to_tensor(s)).wait_recv()
             red[s] = part[s]
-            total = red[0]
+            total = red[0].astype(F32)
             for t in range(1, NS):
-                total = total + red[t]
+                total = total + red[t].astype(F32)
             res[s] = total.astype(BF16)
 
             def send(t, _):
                 to = (s + t) % NS
-                remote(res.at[s], res.at[s], ssem2.at[t], rsem2, to_tensor(to)).start()
+                remote(res.at[s], res.at[s], ssem2, rsem2, to_tensor(to)).start()
                 return 0
 
             lax.fori_loop(1, NS, send, 0)
@@ -293,18 +314,15 @@
         pl.when(s >= many)(lambda: go(ref))
 
     def gather_wait(res, ssem2, rsem2):
-        each_way(res, lambda r: remote(r, r, ssem2.at[0], rsem2, to_tensor(s)).wait_recv())
+        each_way(res, lambda r: remote(r, r, ssem2, rsem2, to_tensor(s)).wait_recv())
 
     def sent(part, res, ssem, ssem2):
         each_way(part, lambda r: remote(r, r, ssem, ssem, to_tensor(s)).wait_send())
 
         @pl.when(s < res.shape[0])
         def _():
-            def one(t, _):
-                remote(res.at[s], res.at[s], ssem2.at[t], ssem2.at[t], to_tensor(s)).wait_send()
-                return 0
-
-            lax.fori_loop(1, NS, one, 0)
+            copies = red1.at[pl.ds(0, NS - 1), pl.ds(0, res.shape[1])]
+            remote(copies, copies, ssem2, ssem2, to_tensor(s)).wait_send()
 
     def slab(ref, i):
         per = ref.shape[1] // RK
@@ -367,7 +385,7 @@
     quarter = unit * 12 / 14
     for i, (d, j) in enumerate(lane):
         for sign in (1, -1):
-            events.append((3.5 + quarter * (i + 1) + (3.0 if i >= 11 else 0.0), "d", (-sign * (d + 1), j if sign > 0 else j ^ 1)))
+            events.append((3.5 + quarter * (i + 1) + (1.5 if i >= 11 else 0.0), "d", (-sign * (d + 1), j if sign > 0 else j ^ 1)))
     passed = [max(e[0] for e in events if e[1] == "d" and e[2][1] // 2 == p) for p in range(2)]
     ready = {}
     for now, what, a in events:
@@ -377,8 +395,6 @@
     last_hop = max(e[0] for e in events if e[1] == "w" and len(weight_hops(*e[2])[1]) > 0)
     ready[(0, 0)] = 0.0
 
-    pass_done = cwait()
-
     def start_ranks():
         scatter(part1, red1, rs1s, rs1r)
 
@@ -402,21 +418,30 @@
     pieces += [(11.0 + 3.0 * n, lambda n=n: ranks(n)) for n in range(NB)]
     pieces += [(29.5, picker), (32.0, masks)]
     begun = (passed[0] + 5.0, passed[1] + 3.0)
-    pieces += [(begun[p], lambda p=p: pass_done(p)) for p in range(2)]
+    pieces += [(begun[0], lambda: cwait(0)), (begun[1], lambda: cwait(2))]
     pieces += [(begun[0] + 0.1, start_ranks), (passed[1] + 0.1, reduce1)]
     pieces += [(last_hop + 1.4, down_packets), (last_hop + 1.5, down_out)]
     by_time = [o for o, _ in sorted(ready.items(), key=lambda kv: (kv[1], kv[0]))]
-    first = [(ox, (0, 1, 0)) for ox in (0, -1, 1, 2)] + [(0, (2, -3, 0))]
-    second = [(ox, (0, 1, 1)) for ox in (0, -1, 1, 2)] + [(0, (2, -3, 1))]
-    paired = [(ox, oy) for ox in (0, -1, 1, 2) for oy in (0, 1)] + [(0, 2), (0, -1)]
-    orders = [by_time, first + second + [o for o in by_time if o not in paired]]
-    for half in range(2):
-        at = (begun[0], passed[1])[half] + 0.2
-        for i, o in enumerate(orders[half]):
-            at = max(at + 0.5, ready.get(o, 0.0) + 0.1)
-            if half == 1 and i == len(first):
-                at = max(at, begun[1] + 0.1)
-            pieces.append((at, lambda o=o, i=i, half=half: product(o[0], o[1], half, i == 0)))
+    at = begun[0] + 0.2
+    for i, o in enumerate(by_time):
+        at = max(at + 0.62, ready[o] + 0.1)
+        pieces.append((at, lambda o=o, i=i: multiply(piece_at(*o), 0, i == 0)))
+    half_near = max(e[0] for e in events if e[1] == "d" and e[2][1] > 1 and abs(e[2][0]) < 3)
+    at = max(half_near + 3.0, ready[(2, 0)] + 0.5, begun[0] + 7.5)
+
+    def clear():
+        r = slice(half_rows, 2 * half_rows)
+        acc[r, :] = jnp.zeros((half_rows, acc.shape[1]), F32)
+
+    pieces += [(begun[0], clear), (at, lambda: cwait(1))]
+    for dz in (0, 1, -1, 2, -2):
+        for core in range(2):
+            at += 0.6
+            pieces.append((at, lambda dz=dz, core=core: early(dz, core)))
+    at = begun[1] + 0.1
+    for o in by_time:
+        at = max(at + 0.3, ready[o] + 0.1)
+        pieces.append((at, lambda o=o: late(*o)))
     pieces += [(last_hop + 1.6 + 0.1 * n, lambda n=n: adapter_term(n)) for n in range(NB)]
 
     line = [(e[0], i, e[1], e[2]) for i, e in enumerate(events)]
@@ -501,13 +526,13 @@
         V((NS, T, WD), BF16), V((NQ,) + w.shape, BF16), V((T, WD), BF16), V((T, FW), BF16), V((T, FW), BF16),
         V((3, A, RK, WD), BF16), V((3, A, RK, FW), BF16),
         V((T, FW), F32), V((T, FW), F32), V((T, FW), BF16), V((T, FW), F32),
-        V((2 * NB, 2 * RK, RB), F32), V((NS, 2 * RK, RB), F32), V((2 * NB, 2 * RK, RB), BF16),
+        V((2 * NB, 2 * RK, RB), BF16), V((NS, 2 * RK, RB), BF16), V((2 * NB, 2 * RK, RB), BF16),
         V((2 * NB, RK, RB), F32), V((NS, RK, RB), F32), V((2 * NB, RK, RB), BF16),
         V((NQ * RK, T), BF16), V((NQ * RK, T), BF16), V((OWN * RK, NQ * RK), BF16),
         V((NQ, RK, FW + WD), BF16), V((NQ, RK, 2 * FW), BF16), V((NQ, RK, 2 * WD), BF16),
         V((NQ, RK, FW + WD), BF16), V((NQ, RK, 2 * FW), BF16),
         V((T, WD), BF16), V((OWN, RK, WD), F32), V((3, OWN, RK, FW), F32),
-        D((11,)), D((7,)), D, D((32,)), D, D((2,)), D, D((64,)), D, D, D((NS,)), D, D, D, D((NS,)), D, D((3,)), D((3,)),
+        D((11,)), D((7,)), D, D((32,)), D, D((3,)), D, D((64,)), D, D, D, D, D, D, D, D, D((3,)), D((3,)),
     ]
     ig, gate_out, up_out, down_in, down_out, late, pick = pl.pallas_call(
         lambda *refs: kernel(dims, *refs),

time: 119 us -> 117 us (0.983)
    pallas_call x1, Pallas kernels: 115 us -> 114 us  [shards(): pl.pallas_call(lambda *refs: kernel(dims, *refs), out_shape=outs, in_spec...]
where the time goes in v3:
time: 117 us
  Pallas kernels  116 us (99%)
    pallas_call x1, Pallas kernels, shards(): pl.pallas_call(lambda *refs: kernel(dims, *refs), out_shape=outs, in_spec...  114 us
    pallas_call x1, Pallas kernels, shards(): pl.pallas_call(finish, out_shape=(flat, wide, tall, wide, tall, tall, wid...  2.51 us

profile of v3, /device:TPU:1, one launch (start us, length us, event | category | flops | bytes accessed | tf_op | source)
XLA Modules:
  0.0 116.9 jit_solution(10660346484443367973)
XLA Ops:
  0.6 113.6 %step.1 = (bf16[768,512]{1,0:T(8,128)(2,1)}, f32[3,16,896]{2,1,0:T(8,128)}, f32[3,16,896]{2,1,0:T(8,128)}, f32[3,16,896]{2,1,0:T(8,128)}, f32[3,16,512]{2,1,0:T(...) custom-call(bf16[768,512]{1,0:T(8,128)(2,1)} %refs_0_.1, bf16[768,512]{1,0:T(8,128)(2,1)} %refs_1_.1, ...), custom_call_target="tpu_custom_call" | custom-call | tf_op jit(solution)/shard_map/step/pallas_call | solution.py:537
  114.2 2.5 %finish.1 = (bf16[768,512]{1,0:T(8,128)(2,1)}, f32[3,16,512]{2,1,0:T(8,128)}, f32[3,16,896]{2,1,0:T(8,128)}, f32[3,16,512]{2,1,0:T(8,128)}, f32[3,16,896]{2,1,0:...) custom-call(bf16[768,512]{1,0:T(8,128)(2,1)} %get-tuple-element.14.ig_i, f32[3,16,896]{2,1,0:T(8,128)} %get-tuple-element.15.gout_i, ...), custom_call_target="tpu_custom_call" | custom-call | tf_op jit(solution)/shard_map/finish/pallas_call | solution.py:548

commit v4 on v3

--- a/solution.py
+++ b/solution.py
@@ -420,7 +420,7 @@
     begun = (passed[0] + 5.0, passed[1] + 3.0)
     pieces += [(begun[0], lambda: cwait(0)), (begun[1], lambda: cwait(2))]
     pieces += [(begun[0] + 0.1, start_ranks), (passed[1] + 0.1, reduce1)]
-    pieces += [(last_hop + 1.4, down_packets), (last_hop + 1.5, down_out)]
+    pieces += [(last_hop + 1.4, down_packets), (max(e[0] for e in events if e[1] == "w") + 0.01, down_out)]
     by_time = [o for o, _ in sorted(ready.items(), key=lambda kv: (kv[1], kv[0]))]
     at = begun[0] + 0.2
     for i, o in enumerate(by_time):

time: 117 us -> 117 us (level)
  no operation moved by 1% of the time
where the time goes in v4:
time: 117 us
  Pallas kernels  116 us (99%)
    pallas_call x1, Pallas kernels, shards(): pl.pallas_call(lambda *refs: kernel(dims, *refs), out_shape=outs, in_spec...  113 us
    pallas_call x1, Pallas kernels, shards(): pl.pallas_call(finish, out_shape=(flat, wide, tall, wide, tall, tall, wid...  2.51 us

profile of v4, /device:TPU:1, one launch (start us, length us, event | category | flops | bytes accessed | tf_op | source)
XLA Modules:
  0.0 116.6 jit_solution(14467407763155688517)
XLA Ops:
  0.6 113.3 %step.1 = (bf16[768,512]{1,0:T(8,128)(2,1)}, f32[3,16,896]{2,1,0:T(8,128)}, f32[3,16,896]{2,1,0:T(8,128)}, f32[3,16,896]{2,1,0:T(8,128)}, f32[3,16,512]{2,1,0:T(...) custom-call(bf16[768,512]{1,0:T(8,128)(2,1)} %refs_0_.1, bf16[768,512]{1,0:T(8,128)(2,1)} %refs_1_.1, ...), custom_call_target="tpu_custom_call" | custom-call | tf_op jit(solution)/shard_map/step/pallas_call | solution.py:537
  113.9 2.5 %finish.1 = (bf16[768,512]{1,0:T(8,128)(2,1)}, f32[3,16,512]{2,1,0:T(8,128)}, f32[3,16,896]{2,1,0:T(8,128)}, f32[3,16,512]{2,1,0:T(8,128)}, f32[3,16,896]{2,1,0:...) custom-call(bf16[768,512]{1,0:T(8,128)(2,1)} %get-tuple-element.14.ig_i, f32[3,16,896]{2,1,0:T(8,128)} %get-tuple-element.15.gout_i, ...), custom_call_target="tpu_custom_call" | custom-call | tf_op jit(solution)/shard_map/finish/pallas_call | solution.py:548

commit v5 on v3

--- a/solution.py
+++ b/solution.py
@@ -567,20 +567,20 @@
     loads = [(late_i, late), (pick_i, pick), (ig_i, ig)]
     loads += [(gout_i, tall.at[0]), (uout_i, tall.at[1]), (din_i, tall.at[2]), (dout_i, wide.at[0])]
     loads = [pltpu.make_async_copy(a, b, in_sem.at[i]) for i, (a, b) in enumerate(loads)]
-    for cp in loads:
+    for cp in loads[2:] + loads[:2]:
         cp.start()
     stores = [(wide.at[1], gin_o), (wide.at[2], uin_o), (ig, ig_o)]
     stores += [(tall.at[0], gout_o), (tall.at[1], uout_o), (tall.at[2], din_o), (wide.at[0], dout_o)]
     stores = [pltpu.make_async_copy(a, b, out_sem.at[i]) for i, (a, b) in enumerate(stores)]
+    for i in range(2, 7):
+        loads[i].wait()
+        stores[i].start()
     for i in range(2):
         loads[i].wait()
     d = jnp.dot(pick[...], late[...].reshape(-1, 2 * WD), preferred_element_type=F32)
     wide[1] = d[:, :WD].reshape(-1, RK, WD)
     wide[2] = d[:, WD:].reshape(-1, RK, WD)
     for i in range(2):
-        stores[i].start()
-    for i in range(2, 7):
-        loads[i].wait()
         stores[i].start()
     for cp in stores:
         cp.wait()

time: 117 us -> 117 us (level)
  no operation moved by 1% of the time
where the time goes in v5:
time: 117 us
  Pallas kernels  116 us (99%)
    pallas_call x1, Pallas kernels, shards(): pl.pallas_call(lambda *refs: kernel(dims, *refs), out_shape=outs, in_spec...  114 us
    pallas_call x1, Pallas kernels, shards(): pl.pallas_call(finish, out_shape=(flat, wide, tall, wide, tall, tall, wid...  2.48 us

profile of v5, /device:TPU:1, one launch (start us, length us, event | category | flops | bytes accessed | tf_op | source)
XLA Modules:
  0.0 116.8 jit_solution(9945529465619034523)
XLA Ops:
  0.6 113.6 %step.1 = (bf16[768,512]{1,0:T(8,128)(2,1)}, f32[3,16,896]{2,1,0:T(8,128)}, f32[3,16,896]{2,1,0:T(8,128)}, f32[3,16,896]{2,1,0:T(8,128)}, f32[3,16,512]{2,1,0:T(...) custom-call(bf16[768,512]{1,0:T(8,128)(2,1)} %refs_0_.1, bf16[768,512]{1,0:T(8,128)(2,1)} %refs_1_.1, ...), custom_call_target="tpu_custom_call" | custom-call | tf_op jit(solution)/shard_map/step/pallas_call | solution.py:537
  114.2 2.5 %finish.1 = (bf16[768,512]{1,0:T(8,128)(2,1)}, f32[3,16,512]{2,1,0:T(8,128)}, f32[3,16,896]{2,1,0:T(8,128)}, f32[3,16,512]{2,1,0:T(8,128)}, f32[3,16,896]{2,1,0:...) custom-call(bf16[768,512]{1,0:T(8,128)(2,1)} %get-tuple-element.14.ig_i, f32[3,16,896]{2,1,0:T(8,128)} %get-tuple-element.15.gout_i, ...), custom_call_target="tpu_custom_call" | custom-call | tf_op jit(solution)/shard_map/finish/pallas_call | solution.py:548
